TPU v7x, 128 devices: a whole 4x4x4 slice. The times are simulated.
128 devices in a mesh: outer: 16 (over x, y), inner: 8 (over z, core).
Axes of the slice: x: 4, y: 4, z: 4, core: 2. Of those that a mesh axis runs over, the one named last changes fastest.
Arguments:
- query_proj: bfloat16 [196608, 2048], P(('outer', 'inner')), may hold values from -6 to 6
- key_proj: bfloat16 [196608, 2048], P(('outer', 'inner')), may hold values from -6 to 6
- value_proj: bfloat16 [196608, 2048], P(('outer', 'inner')), may hold values from -6 to 6
- norm_gain: float32 [2048], replicated, may hold values from 0.25 to 1.75
Outputs:
- attended: bfloat16 [196608, 2048], P(('outer', 'inner'))
All inputs are finite; a program needn't handle non-finite values.
Results may differ from a plain program's by a relative error of at most 0.0049.
Values sent between devices are 32-bit elements; how exact they have to be, the bound alone decides.
No kernel may reach another device: no remote copies, remote signals or barrier semaphores. Data moves between devices by JAX's collectives and lax.ppermute only.
A program may use at most 192 MiB of HBM per device.

v0:
```python
import jax
import jax.numpy as jnp
from jax import lax
from jax.sharding import Mesh
from jax.sharding import PartitionSpec as P

H = 16
DK = 128
SPAN = 256
OUTER = ("outer_0", "outer_1")
OUTER_INNER = ("outer_0", "outer_1", "inner")


def filled_with(array, identity):
    return jnp.zeros_like(array) + jnp.asarray(identity, array.dtype)


def carried_in(array, axes, combine, identity):
    before = start = filled_with(array, identity)
    subtotal = array
    for axis in reversed(axes):
        size, place = (lax.axis_size(axis), lax.axis_index(axis))
        pieces = lax.all_gather(subtotal, axis)
        inside, subtotal = (start, start)
        for k in range(size):
            passed = k < place
            subtotal = combine(subtotal, pieces[k])
            inside = jnp.where(passed, subtotal, inside)
        before = combine(inside, before)
    return before


def add_states(earlier, later):
    return earlier + later


def shards(query_proj, key_proj, value_proj, norm_gain):
    tokens = query_proj.shape[0]
    count = tokens // SPAN
    shape = (count, SPAN, H, DK)
    queries = query_proj.reshape(shape)
    keys_local = key_proj.reshape(shape)
    values_local = value_proj.reshape(shape)
    block_states = jnp.einsum(
        "nchd,nche->nhde", keys_local, values_local, preferred_element_type=jnp.float32
    )
    total = jnp.sum(block_states, axis=0)
    flat = total.reshape(1, H * DK * DK)
    shares = lax.all_to_all(flat, "inner", split_axis=1, concat_axis=0, tiled=True)
    share_within = jnp.cumsum(shares, axis=0) - shares
    share_total = jnp.sum(shares, axis=0)
    share_earlier = carried_in(share_total, OUTER, add_states, jnp.zeros_like(share_total))
    share_prefix = share_within + share_earlier[None]
    mine = lax.all_to_all(share_prefix, "inner", split_axis=0, concat_axis=1, tiled=True)
    prefix = mine.reshape(H, DK, DK)
    running = jnp.cumsum(block_states, axis=0) - block_states
    boundary = (prefix[None] + running).astype(jnp.bfloat16)
    carried = jnp.einsum("nchd,nhde->nche", queries, boundary, preferred_element_type=jnp.float32)
    positions = jnp.arange(SPAN)
    causal = positions[:, None] >= positions[None, :]
    scores = jnp.einsum("nchd,nshd->nhcs", queries, keys_local, preferred_element_type=jnp.float32)
    scores = jnp.where(causal[None, None], scores, 0.0).astype(jnp.bfloat16)
    local = jnp.einsum("nhcs,nshe->nche", scores, values_local, preferred_element_type=jnp.float32)
    raw = carried + local
    meansq = jnp.mean(raw * raw, axis=-1, keepdims=True)
    normed = raw * lax.rsqrt(meansq + 1e-06) * norm_gain.reshape(H, DK)
    return normed.astype(jnp.bfloat16).reshape(tokens, H * DK)


def solution(mesh):
    finer = Mesh(mesh.devices.reshape(4, 4, mesh.shape["inner"]), ("outer_0", "outer_1", "inner"))
    placed = (P(OUTER_INNER, None), P(OUTER_INNER, None), P(OUTER_INNER, None), P())
    return jax.shard_map(
        shards, mesh=finer, in_specs=placed, out_specs=P(OUTER_INNER, None), check_vma=False
    )
```

profile of v0, /device:TPU:1, one launch (start us, length us, event | category | flops | bytes accessed | tf_op | source)
XLA Modules:
  0.0 169.4 jit_solution(1092509162153517310)
XLA Ops:
  0.0 7.8 %copy.26 = bf16[192,8,16,128]{3,2,1,0:T(8,128)(2,1)} copy(bf16[192,8,16,128]{3,1,2,0:T(8,128)(2,1)} %bitcast.52) | data formatting | bytes 12582912
  7.8 9.0 %copy.22 = bf16[6,256,16,128]{1,3,2,0:T(8,128)(2,1)} copy(bf16[6,256,16,128]{3,2,1,0:T(8,128)(2,1)} %bitcast.49) | data formatting | bytes 12582912 | tf_op jit(solution)/shard_map/reshape | solution.py:43
  16.9 7.8 %copy.25 = bf16[192,8,16,128]{3,2,1,0:T(8,128)(2,1)} copy(bf16[192,8,16,128]{3,1,2,0:T(8,128)(2,1)} %bitcast.53) | data formatting | bytes 12582912
  24.7 10.6 %fusion.19 = (f32[16,128,128]{2,1,0:T(8,128)}, f32[6,16,128,128]{3,2,1,0:T(8,128)}) fusion(bf16[6,256,16,128]{1,3,2,0:T(8,128)(2,1)} %copy.22, bf16[6,256,16,128]{3,2,1,0:T(8,128)(2,1)} %bitcast.46), kind=kOutput, calls=%fused_computation.36 | convolution fusion | flops 806617088 | bytes 19922944 | tf_op jit(solution)/shard_map/nchd,nche->nhde/dot_general | solution.py:44
  35.3 6.8 %all-to-all-start = ((f32[1,8,32768]{2,0,1:T(1,128)}), f32[1,8,32768]{2,0,1:T(1,128)S(1)}, u32[]{:S(2)}, u32[]{:S(2)}) async-start(f32[1,8,32768]{2,0,1:T(1,128)} %bitcast), calls=%async_computation | async-start | bytes 2097152 | tf_op jit(solution)/shard_map/all_to_all | solution.py:49
  42.1 15.0 %all-to-all-done = f32[1,8,32768]{2,0,1:T(1,128)S(1)} async-done(((f32[1,8,32768]{2,0,1:T(1,128)}), f32[1,8,32768]{2,0,1:T(1,128)S(1)}, u32[]{:S(2)}, u32[]{:S(2)}) %all-to-all-start) | async-done | bytes 1048608 | tf_op jit(solution)/shard_map/all_to_all | solution.py:49
  57.1 0.8 reduce_sum.28
  57.9 11.8 %all-gather = f32[131072]{0:T(1024)S(1)} all-gather(f32[32768]{0:T(1024)S(1)} %reduce_sum.28), channel_id=2, replica_groups=mesh['outer_0'=4,'outer_1'=4,'inner'=8] {'outer_1'}, dimensions={0}, use_global_device_ids=true | all-gather | bytes 655360 | tf_op jit(solution)/shard_map/all_gather | solution.py:23
  69.7 10.4 %all-gather.1 = f32[4,1,32768]{2,1,0:T(1,128)S(1)} all-gather(f32[1,1,32768]{2,1,0:T(1,128)S(1)} %bitcast.56), channel_id=1, replica_groups=mesh['outer_0'=4,'outer_1'=4,'inner'=8] {'outer_0'}, dimensions={0}, use_global_device_ids=true | all-gather | bytes 655360 | tf_op jit(solution)/shard_map/all_gather | solution.py:23
  80.1 0.3 fusion.16
  80.4 1.8 %fusion = f32[8,1,32768]{2,1,0:T(1,128)} fusion(f32[1,8,32768]{2,0,1:T(1,128)S(1)} %all-to-all-done, f32[32768]{0:T(1024)S(1)} %bitcast.57), kind=kOutput, calls=%fused_computation.1 | output fusion | flops 2359296 | bytes 2228224 | tf_op jit(solution)/shard_map/jit(cumsum)/reduce_window_sum | solution.py:50
  82.3 0.0 slice-start
  82.3 9.4 %all-to-all-start.1 = ((f32[8,1,32768]{2,1,0:T(1,128)}), f32[8,1,32768]{2,1,0:T(1,128)S(1)}, u32[]{:S(2)}, u32[]{:S(2)}) async-start(f32[8,1,32768]{2,1,0:T(1,128)} %fusion), calls=%async_computation.1 | async-start | bytes 2097152 | tf_op jit(solution)/shard_map/all_to_all | solution.py:54
  91.7 0.0 slice-start.1
  91.7 8.0 %copy.27 = bf16[192,8,16,128]{3,2,1,0:T(8,128)(2,1)} copy(bf16[192,8,16,128]{3,1,2,0:T(8,128)(2,1)} %bitcast.54) | data formatting | bytes 12582912
  99.7 0.0 slice-done
  99.7 0.0 slice-done.1
  99.7 3.2 %fusion.24 = f32[6,16,128,128]{3,2,1,0:T(8,128)} fusion(f32[6,16,128,128]{3,2,1,0:T(8,128)S(1)} %bitcast.45), kind=kOutput, calls=%fused_computation.37 | output fusion | flops 7864320 | bytes 12582912 | tf_op jit(solution)/shard_map/jit(cumsum)/reduce_window_sum | solution.py:56
  102.9 3.7 %all-to-all-done.1 = f32[8,1,32768]{2,1,0:T(1,128)S(1)} async-done(((f32[8,1,32768]{2,1,0:T(1,128)}), f32[8,1,32768]{2,1,0:T(1,128)S(1)}, u32[]{:S(2)}, u32[]{:S(2)}) %all-to-all-start.1) | async-done | bytes 1048608 | tf_op jit(solution)/shard_map/all_to_all | solution.py:54
  106.7 13.6 %fusion.12 = f32[6,16,128,256]{3,2,1,0:T(8,128)} fusion(bf16[6,256,16,128]{3,2,1,0:T(8,128)(2,1)} %bitcast.50, f32[6,16,128,128]{3,2,1,0:T(8,128)} %fusion.24, f32[6,16,128,128]{3,2,1,0:T(8,128)} %get-tuple-element.8, f32[16,128,128]{2,1,0:T(8,128)S(1)} %bitcast.55), kind=kOutput, calls=%fused_computation.16 | convolution fusion | flops 810024960 | bytes 32505856 | tf_op jit(solution)/shard_map/nchd,nhde->nche/dot_general | solution.py:58
  120.2 0.0 copy-start
  120.2 19.4 %multiply_reduce_fusion = (f32[6,256,16]{1,2,0:T(8,128)S(1)}, f32[6,16,256,128]{2,3,1,0:T(8,128)}) fusion(f32[6,16,128,256]{3,2,1,0:T(8,128)} %fusion.12, bf16[6,256,16,128]{1,3,2,0:T(8,128)(2,1)} %copy.22, pred[256,256]{1,0:T(8,128)(4,1)S(1)} %iota_compare_fusion, bf16[6,256,16,128]{3,2,1,0:T(8,128)(2,1)} %bitcast.47, bf16[6,256,16,128]{3,2,1,0:T(8,128)(2,1)} %bitcast.51), kind=kOutput, calls=%fused_computation.6 | convolution fusion | flops 3243220992 | bytes 44204032 | tf_op jit(solution)/shard_map/nhcs,nshe->nche/dot_general | solution.py:63
  139.7 0.0 copy-done
  139.7 12.0 %multiply_convert_fusion = bf16[6,256,16,128]{1,3,2,0:T(8,128)(2,1)} fusion(f32[16,128]{1,0:T(8,128)S(1)} %bitcast.59, f32[6,256,16]{1,2,0:T(8,128)S(1)} %add_rsqrt_fusion, f32[6,16,256,128]{2,3,1,0:T(8,128)} %get-tuple-element.10, f32[6,16,128,256]{3,2,1,0:T(8,128)} %fusion.12), kind=kLoop, calls=%fused_computation.5 | loop fusion | flops 12582912 | bytes 31563776 | tf_op jit(solution)/shard_map/convert_element_type | solution.py:67
  151.6 9.1 %copy.23 = bf16[6,256,16,128]{3,2,1,0:T(8,128)(2,1)} copy(bf16[6,256,16,128]{1,3,2,0:T(8,128)(2,1)} %multiply_convert_fusion) | data formatting | bytes 12582912 | tf_op jit(solution)/shard_map/convert_element_type | solution.py:67
  160.7 8.7 %copy.46 = bf16[192,8,16,128]{3,1,2,0:T(8,128)(2,1)} copy(bf16[192,8,16,128]{3,2,1,0:T(8,128)(2,1)} %bitcast.48) | data formatting | bytes 12582912
  (4 shorter events, 0.1 us)
Async XLA Ops:
  35.3 21.8 %all-to-all-start = ((f32[1,8,32768]{2,0,1:T(1,128)}), f32[1,8,32768]{2,0,1:T(1,128)S(1)}, u32[]{:S(2)}, u32[]{:S(2)}) async-start(f32[1,8,32768]{2,0,1:T(1,128)} %bitcast), calls=%async_computation | async-start | bytes 2097152 | tf_op jit(solution)/shard_map/all_to_all | solution.py:49
  82.3 17.4 %slice-start = ((s8[6291456]{0:T(1024)(128)(4,1)}), s8[2097152]{0:T(1024)(128)(4,1)S(1)}, s32[]{:S(2)}) async-start(s8[6291456]{0:T(1024)(128)(4,1)} %bitcast.44), calls=%async_computation.2 | async-start | bytes 4194304
  82.3 24.4 %all-to-all-start.1 = ((f32[8,1,32768]{2,1,0:T(1,128)}), f32[8,1,32768]{2,1,0:T(1,128)S(1)}, u32[]{:S(2)}, u32[]{:S(2)}) async-start(f32[8,1,32768]{2,1,0:T(1,128)} %fusion), calls=%async_computation.1 | async-start | bytes 2097152 | tf_op jit(solution)/shard_map/all_to_all | solution.py:54
  91.7 8.0 %slice-start.1 = ((s8[6291456]{0:T(1024)(128)(4,1)}), s8[4194304]{0:T(1024)(128)(4,1)S(1)}, s32[]{:S(2)}) async-start(s8[6291456]{0:T(1024)(128)(4,1)} %bitcast.44), calls=%async_computation.3 | async-start | bytes 8388608
  120.2 19.5 %copy-start = (f32[2048]{0:T(1024)S(1)}, f32[2048]{0:T(1024)}, u32[]{:S(2)}) copy-start(f32[2048]{0:T(1024)} %param.7) | copy-start | bytes 24580
where the time goes:
time: 170 us; the launch traced here: 169 us
  local copies, waits for them, and re-layouts  50.5 us (30%)
  matrix products  43.6 us (26%)
  blocking collectives  22.2 us (13%)
  waiting for transfers between devices  18.7 us (11%)
  other arithmetic  18.2 us (11%)
  starting transfers between devices  16.2 us (10%)
    unnamed x10, local copies, waits for them, and re-layouts  32.4 us
    all_gather x2, blocking collectives, carried_in(): pieces = lax.all_gather(subtotal, axis)  22.2 us
    dot_general x1, matrix products, shards(): jnp.einsum('nhcs,nshe->nche', scores, values_local, preferred_element_typ...  19.4 us
    all_to_all x1, waiting for transfers between devices, shards(): lax.all_to_all(flat, 'inner', split_axis=1, concat_axis=0, tiled=True)  15 us
    dot_general x1, matrix products, shards(): jnp.einsum('nchd,nhde->nche', queries, boundary, preferred_element_type=j...  13.6 us
    convert_element_type x1, other arithmetic, shards(): return normed.astype(jnp.bfloat16).reshape(tokens, H * DK)  12 us
    dot_general x1, matrix products, shards(): jnp.einsum('nchd,nche->nhde', keys_local, values_local, preferred_element...  10.6 us
    all_to_all x1, starting transfers between devices, shards(): lax.all_to_all(share_prefix, 'inner', split_axis=0, concat_axis=1, tiled=...  9.38 us
  transfers between devices with their start and end apart: 2, of which 2 were waited for; matrix products, arithmetic and copies ran while one was open for 7% of the time, Pallas kernels for 0%

commit v1 on v0

v1 whole, which is shorter than its diff:
```python
import functools

import jax
import jax.numpy as jnp
from jax import lax
from jax.experimental import pallas as pl
from jax.experimental.pallas import tpu as pltpu
from jax.sharding import Mesh
from jax.sharding import PartitionSpec as P

H = 16
DK = 128
SPAN = 256
HALF = H // 2
CHIPS = ("x", "y", "z")
ALL = ("x", "y", "z", "c")
PAIR = 2 * DK
F32 = jnp.float32
BF16 = jnp.bfloat16


def in_hbm(array):
    return pltpu.with_memory_space_constraint(array, pltpu.HBM)


def state_kernel(half_ref, k_ref, v_ref, o_ref):
    for h in range(2):
        cols = slice(h * DK, (h + 1) * DK)
        o_ref[cols, :] = lax.dot_general(
            k_ref[:, cols], v_ref[:, cols], (((0,), (0,)), ((), ())), preferred_element_type=F32
        )


def half_states(half, keys, values):
    tokens = keys.shape[0]
    steps = HALF // 2
    block = pl.BlockSpec((tokens, PAIR), lambda i, half: (0, half[0] * steps + i))
    return pl.pallas_call(
        state_kernel,
        out_shape=jax.ShapeDtypeStruct((HALF * DK, DK), F32),
        grid_spec=pltpu.PrefetchScalarGridSpec(
            num_scalar_prefetch=1,
            grid=(steps,),
            in_specs=[block, block],
            out_specs=pl.BlockSpec((PAIR, DK), lambda i, half: (i, 0)),
        ),
        compiler_params=pltpu.CompilerParams(vmem_limit_bytes=16 * 2**20),
        cost_estimate=pl.CostEstimate(
            flops=2 * tokens * HALF * DK * DK, bytes_accessed=4 * tokens * HALF * DK, transcendentals=0
        ),
        name="half_states",
    )(half, in_hbm(keys), in_hbm(values))


def local_kernel(q_ref, k_ref, v_ref, o_ref):
    count = q_ref.shape[0] // SPAN
    rows = lax.broadcasted_iota(jnp.int32, (SPAN, SPAN), 0)
    cols = lax.broadcasted_iota(jnp.int32, (SPAN, SPAN), 1)
    causal = rows >= cols
    for h in range(2):
        lanes = slice(h * DK, (h + 1) * DK)
        running = None
        for n in range(count):
            span = slice(n * SPAN, (n + 1) * SPAN)
            q, k, v = q_ref[span, lanes], k_ref[span, lanes], v_ref[span, lanes]
            scores = lax.dot_general(q, k, (((1,), (1,)), ((), ())), preferred_element_type=F32)
            scores = jnp.where(causal, scores, 0.0).astype(BF16)
            out = jnp.dot(scores, v, preferred_element_type=F32)
            if n:
                out += jnp.dot(q, running.astype(BF16), preferred_element_type=F32)
            if n < count - 1:
                state = lax.dot_general(k, v, (((0,), (0,)), ((), ())), preferred_element_type=F32)
                running = state if running is None else running + state
            o_ref[span, lanes] = out


def local_part(queries, keys, values):
    tokens, width = queries.shape
    block = pl.BlockSpec((tokens, PAIR), lambda i: (0, i))
    return pl.pallas_call(
        local_kernel,
        out_shape=pltpu.HBM((tokens, width), F32),
        grid=(width // PAIR,),
        in_specs=[block, block, block],
        out_specs=block,
        compiler_params=pltpu.CompilerParams(vmem_limit_bytes=32 * 2**20),
        cost_estimate=pl.CostEstimate(
            flops=6 * tokens * width * SPAN, bytes_accessed=10 * tokens * width, transcendentals=0
        ),
        name="local_part",
    )(in_hbm(queries), in_hbm(keys), in_hbm(values))


def scan_kernel(x_ref, o_ref):
    total = jnp.zeros(x_ref.shape[1:], F32)
    for j in range(x_ref.shape[0]):
        o_ref[j] = total
        total += x_ref[j]


def earlier_sums(x):
    return pl.pallas_call(
        scan_kernel,
        out_shape=jax.ShapeDtypeStruct(x.shape, x.dtype),
        compiler_params=pltpu.CompilerParams(vmem_limit_bytes=4 * 2**20),
        name="earlier_sums",
    )(x)


def core_kernel(core_ref, chip_ref, mine_ref, theirs_ref, own_ref, partner_ref):
    first = chip_ref[...]

    @pl.when(core_ref[0] == 0)
    def _():
        own_ref[...] = first
        partner_ref[...] = first + mine_ref[...]

    @pl.when(core_ref[0] == 1)
    def _():
        own_ref[...] = first + theirs_ref[...]
        partner_ref[...] = first


def core_prefixes(core, before_chip, mine, theirs):
    whole = pl.BlockSpec(memory_space=pltpu.VMEM)
    return pl.pallas_call(
        core_kernel,
        out_shape=[jax.ShapeDtypeStruct(before_chip.shape, F32)] * 2,
        in_specs=[pl.BlockSpec(memory_space=pltpu.SMEM), whole, whole, whole],
        out_specs=[whole, whole],
        compiler_params=pltpu.CompilerParams(vmem_limit_bytes=8 * 2**20),
        name="core_prefixes",
    )(core, before_chip, mine, theirs)


def output_kernel(half_ref, q_ref, local_ref, prefix_ref, gain_ref, *rest):
    o_ref = rest[-1]
    ones = jnp.full((DK, DK), 1.0 / DK, BF16)
    for h in range(2):
        lanes = slice(h * DK, (h + 1) * DK)
        prefix = prefix_ref[lanes, :].astype(BF16)
        gain = gain_ref[:, lanes]
        for n in range(q_ref.shape[0] // SPAN):
            span = slice(n * SPAN, (n + 1) * SPAN)
            raw = local_ref[span, lanes] + jnp.dot(q_ref[span, lanes], prefix, preferred_element_type=F32)
            meansq = jnp.dot((raw * raw).astype(BF16), ones, preferred_element_type=F32)
            o_ref[span, lanes] = (raw * lax.rsqrt(meansq + 1e-06) * gain).astype(BF16)


def half_output(half, queries, local, prefix, gain, partial):
    tokens, width = queries.shape
    steps = HALF // 2
    block = pl.BlockSpec((tokens, PAIR), lambda i, half: (0, half[0] * steps + i))
    in_specs = [
        block,
        block,
        pl.BlockSpec((PAIR, DK), lambda i, half: (i, 0)),
        pl.BlockSpec((1, PAIR), lambda i, half: (0, half[0] * steps + i)),
    ]
    args = [half, in_hbm(queries), in_hbm(local), prefix, gain]
    alias = {}
    if partial is not None:
        in_specs.append(pl.BlockSpec(memory_space=pl.ANY))
        args.append(partial)
        alias = {5: 0}
    return pl.pallas_call(
        output_kernel,
        out_shape=jax.ShapeDtypeStruct((tokens, width), BF16),
        grid_spec=pltpu.PrefetchScalarGridSpec(
            num_scalar_prefetch=1, grid=(steps,), in_specs=in_specs, out_specs=block
        ),
        input_output_aliases=alias,
        compiler_params=pltpu.CompilerParams(vmem_limit_bytes=24 * 2**20),
        cost_estimate=pl.CostEstimate(
            flops=4 * tokens * HALF * DK * DK, bytes_accessed=8 * tokens * HALF * DK, transcendentals=0
        ),
        name="half_output",
    )(*args)


def shards(queries, keys, values, norm_gain):
    core = lax.axis_index("c")
    own = core.astype(jnp.int32).reshape(1)
    other = 1 - own
    swap = functools.partial(lax.ppermute, axis_name="c", perm=[(0, 1), (1, 0)])
    theirs = swap(half_states(other, keys, values))
    mine = half_states(own, keys, values)
    chip = mine + theirs
    chips = lax.axis_size("x") * lax.axis_size("y") * lax.axis_size("z")
    pieces = lax.all_to_all(chip, CHIPS, 0, 0, tiled=True)
    local = local_part(queries, keys, values)
    sums = earlier_sums(pieces.reshape(chips, -1, DK)).reshape(pieces.shape)
    before_chip = lax.all_to_all(sums, CHIPS, 0, 0, tiled=True)
    prefix_own, prefix_partner = core_prefixes(own, before_chip, mine, theirs)
    prefix_other = swap(prefix_partner)
    gain = norm_gain.reshape(1, -1)
    out = half_output(own, queries, local, prefix_own, gain, None)
    return half_output(other, queries, local, prefix_other, gain, out)


def solution(mesh):
    finer = Mesh(mesh.devices.reshape(4, 4, mesh.shape["inner"] // 2, 2), ALL)
    return jax.shard_map(
        shards, mesh=finer, in_specs=(P(ALL, None),) * 3 + (P(),), out_specs=P(ALL, None), check_vma=False
    )
```

time: 170 us -> 84.4 us (0.50)
  local copies, waits for them, and re-layouts: 50.5 us -> 0.01 us
  matrix products: 43.6 us -> 0 us
  Pallas kernels: 0 us -> 40.4 us
  waiting for transfers between devices: 18.7 us -> 0.01 us
  other arithmetic: 18.2 us -> 0.06 us
  blocking collectives: 22.2 us -> 38.8 us
  starting transfers between devices: 16.2 us -> 4.58 us
    dot_general x3 -> x0, matrix products: 43.6 us -> none  [the longest x1 19.4 us: shards(): jnp.einsum('nhcs,nshe->nche', scores, values_local, preferred_element_typ...]
    pallas_call x0 -> x7, Pallas kernels: none -> 40.4 us  [the longest x1 17.7 us: local_part(): pl.pallas_call(local_kernel, out_shape=pltpu.HBM((tokens, width), F32), g...]
    all_to_all x0 -> x2, blocking collectives: none -> 38.8 us  [the longest x1 23.1 us: shards(): pieces = lax.all_to_all(chip, CHIPS, 0, 0, tiled=True)]
    unnamed x10 -> x2, local copies, waits for them, and re-layouts: 32.4 us -> 0.01 us
    all_gather x2 -> x0, blocking collectives: 22.2 us -> none  [carried_in(): pieces = lax.all_gather(subtotal, axis)]
    all_to_all x2 -> x0, waiting for transfers between devices: 18.7 us -> none  [the longest x1 15 us: shards(): lax.all_to_all(flat, 'inner', split_axis=1, concat_axis=0, tiled=True)]
    all_to_all x2 -> x0, starting transfers between devices: 16.2 us -> none  [the longest x1 9.38 us: shards(): lax.all_to_all(share_prefix, 'inner', split_axis=0, concat_axis=1, tiled=...]
    convert_element_type x1 -> x0, other arithmetic: 12 us -> none  [shards(): return normed.astype(jnp.bfloat16).reshape(tokens, H * DK)]
  transfers between devices with their start and end apart: 2 -> 2, of which waited for: 2 -> 0; matrix products, arithmetic and copies ran while one was open for 7% -> 0% of each run, Pallas kernels for 0% -> 35%
where the time goes in v1:
time: 84.4 us; the launch traced here: 83.8 us
  Pallas kernels  40.4 us (48%)
  blocking collectives  38.8 us (46%)
  starting transfers between devices  4.58 us (5%)
    all_to_all x1, blocking collectives, shards(): pieces = lax.all_to_all(chip, CHIPS, 0, 0, tiled=True)  23.1 us
    pallas_call x1, Pallas kernels, local_part(): pl.pallas_call(local_kernel, out_shape=pltpu.HBM((tokens, width), F32), g...  17.7 us
    all_to_all x1, blocking collectives, shards(): before_chip = lax.all_to_all(sums, CHIPS, 0, 0, tiled=True)  15.6 us
    pallas_call x2, Pallas kernels, half_output(): pl.pallas_call(output_kernel, out_shape=jax.ShapeDtypeStruct((tokens, wid...  13.9 us
    pallas_call x2, Pallas kernels, half_states(): pl.pallas_call(state_kernel, out_shape=jax.ShapeDtypeStruct((HALF * DK, D...  8.53 us
    ppermute x1, starting transfers between devices, shards(): prefix_other = swap(prefix_partner)  3.21 us
  transfers between devices with their start and end apart: 2, of which 0 were waited for; matrix products, arithmetic and copies ran while one was open for 0% of the time, Pallas kernels for 35%

profile of v1, /device:TPU:1, one launch (start us, length us, event | category | flops | bytes accessed | tf_op | source)
XLA Modules:
  0.0 83.8 jit_solution(14294059648488491741)
XLA Ops:
  0.0 4.3 %half_states.3 = f32[1024,128]{1,0:T(8,128)S(1)} custom-call(s32[1]{0:T(128)S(6)} %sub.3.half_ref, bf16[1536,2048]{1,0:T(8,128)(2,1)} %k_ref.5, bf16[1536,2048]{1,0:T(8,128)(2,1)} %v_ref.5), custom_call_target="tpu_custom_call" | custom-call | flops 402653184 | bytes 6291456 | tf_op jit(solution)/shard_map/half_states/pallas_call | solution.py:38
  4.3 1.4 %collective-permute-start = (f32[1024,128]{1,0:T(8,128)S(1)}, f32[1024,128]{1,0:T(8,128)S(1)}, u32[]{:S(2)}, u32[]{:S(2)}) collective-permute-start(f32[1024,128]{1,0:T(8,128)S(1)} %half_states.3), channel_id=1, source_target_pairs={{0,1},{1,0},{2,3},{3,2},{4,5},{5,4},{6,7},{7,6},{8,9},{9,8},{10,11... | collective-permute-start | bytes 1572872 | tf_op jit(solution)/shard_map/ppermute | solution.py:186
  5.7 4.2 %half_states.2.mine_ref = f32[1024,128]{1,0:T(8,128)S(1)} custom-call(s32[1]{0:T(128)} %bitcast.half_ref.core_ref, bf16[1536,2048]{1,0:T(8,128)(2,1)} %k_ref.5, bf16[1536,2048]{1,0:T(8,128)(2,1)} %v_ref.5), custom_call_target="tpu_custom_call" | custom-call | flops 402653184 | bytes 6291456 | tf_op jit(solution)/shard_map/half_states/pallas_call | solution.py:38
  9.9 0.0 collective-permute-done.theirs_ref
  9.9 0.1 add.3
  10.0 23.1 %all_to_all.17.x_ref = f32[64,16,128]{2,1,0:T(8,128)S(1)} all-to-all(f32[64,16,128]{2,1,0:T(8,128)S(1)} %bitcast.7), channel_id=1, replica_groups=mesh['x'=4,'y'=4,'z'=4,'c'=2] {'x','y','z'}, dimensions={0} | all-to-all | bytes 1048576 | tf_op jit(solution)/shard_map/all_to_all | solution.py:190
  33.1 0.1 earlier_sums.1
  33.2 15.6 %all_to_all.18 = f32[64,16,128]{2,1,0:T(8,128)S(1)} all-to-all(f32[64,16,128]{2,1,0:T(8,128)S(1)} %earlier_sums.1), channel_id=1, replica_groups=mesh['x'=4,'y'=4,'z'=4,'c'=2] {'x','y','z'}, dimensions={0} | all-to-all | bytes 1048576 | tf_op jit(solution)/shard_map/all_to_all | solution.py:193
  48.9 0.1 core_prefixes.1
  49.0 0.0 copy-start
  49.0 3.2 %collective-permute-start.1 = (f32[1024,128]{1,0:T(8,128)S(1)}, f32[1024,128]{1,0:T(8,128)S(1)}, u32[]{:S(2)}, u32[]{:S(2)}) collective-permute-start(f32[1024,128]{1,0:T(8,128)S(1)} %get-tuple-element.7), channel_id=1, source_target_pairs={{0,1},{1,0},{2,3},{3,2},{4,5},{5,4},{6,7},{7,6},{8,9},{9,8},{10,11... | collective-permute-start | bytes 1572872 | tf_op jit(solution)/shard_map/ppermute | solution.py:195
  52.2 17.7 %local_part.1.local_ref = f32[1536,2048]{1,0:T(8,128)} custom-call(bf16[1536,2048]{1,0:T(8,128)(2,1)} %q_ref.5, bf16[1536,2048]{1,0:T(8,128)(2,1)} %k_ref.5, bf16[1536,2048]{1,0:T(8,128)(2,1)} %v_ref.5), custom_call_target="tpu_custom_call" | custom-call | flops 4831838208 | bytes 31457280 | tf_op jit(solution)/shard_map/local_part/pallas_call | solution.py:80
  69.9 0.0 copy-done
  69.9 7.0 %half_output.2.rest_0_ = bf16[1536,2048]{1,0:T(8,128)(2,1)} custom-call(s32[1]{0:T(128)} %bitcast.half_ref.core_ref, bf16[1536,2048]{1,0:T(8,128)(2,1)} %q_ref.5, f32[1536,2048]{1,0:T(8,128)} %local_part.1.local_ref, f32[1024,128]{1,0:T(8,128)S(1)} %get-tuple-element.8.prefix_ref, f32[1,2048]{1,0:T(1,128)S(1)} %bitcast.5), custom_call_target="tpu_custom_call" | custom-call | flops 805306368 | bytes 12582912 | tf_op jit(solution)/shard_map/half_output/pallas_call | solution.py:166
  76.9 0.0 collective-permute-done.1.prefix_ref
  76.9 7.0 %half_output.3 = bf16[1536,2048]{1,0:T(8,128)(2,1)} custom-call(s32[1]{0:T(128)S(6)} %sub.3.half_ref, bf16[1536,2048]{1,0:T(8,128)(2,1)} %q_ref.5, f32[1536,2048]{1,0:T(8,128)} %local_part.1.local_ref, f32[1024,128]{1,0:T(8,128)S(1)} %collective-permute-done.1.prefix_ref, f32[1,2048]{1,0:T(1,128)S(1)} %bitcast.6, ...), custom_call_target="tpu_custom_call", output_to_operand_aliasing={{}: (5, {})} | custom-call | flops 805306368 | bytes 12582912 | tf_op jit(solution)/shard_map/half_output/pallas_call | solution.py:166
Async XLA Ops:
  4.3 5.6 %collective-permute-start = (f32[1024,128]{1,0:T(8,128)S(1)}, f32[1024,128]{1,0:T(8,128)S(1)}, u32[]{:S(2)}, u32[]{:S(2)}) collective-permute-start(f32[1024,128]{1,0:T(8,128)S(1)} %half_states.3), channel_id=1, source_target_pairs={{0,1},{1,0},{2,3},{3,2},{4,5},{5,4},{6,7},{7,6},{8,9},{9,8},{10,11... | collective-permute-start | bytes 1572872 | tf_op jit(solution)/shard_map/ppermute | solution.py:186
  49.0 21.0 %copy-start = (f32[2048]{0:T(1024)S(1)}, f32[2048]{0:T(1024)}, u32[]{:S(2)}) copy-start(f32[2048]{0:T(1024)} %param.7) | copy-start | bytes 24580
  49.0 27.9 %collective-permute-start.1 = (f32[1024,128]{1,0:T(8,128)S(1)}, f32[1024,128]{1,0:T(8,128)S(1)}, u32[]{:S(2)}, u32[]{:S(2)}) collective-permute-start(f32[1024,128]{1,0:T(8,128)S(1)} %get-tuple-element.7), channel_id=1, source_target_pairs={{0,1},{1,0},{2,3},{3,2},{4,5},{5,4},{6,7},{7,6},{8,9},{9,8},{10,11... | collective-permute-start | bytes 1572872 | tf_op jit(solution)/shard_map/ppermute | solution.py:195

commit v2 on v0

v2 whole, which is shorter than its diff:
```python
import functools

import jax
import jax.numpy as jnp
from jax import lax
from jax.experimental import pallas as pl
from jax.experimental.pallas import tpu as pltpu
from jax.sharding import Mesh
from jax.sharding import PartitionSpec as P

H = 16
DK = 128
SPAN = 256
HALF = H // 2
CHIPS = ("x", "y", "z")
ALL = ("x", "y", "z", "c")
PAIR = 2 * DK
CHUNKS = HALF // 2
WIDTH = HALF * DK
MIB = 2**20
F32 = jnp.float32
BF16 = jnp.bfloat16
SMEM = pl.BlockSpec(memory_space=pltpu.SMEM)
VMEM = pl.BlockSpec(memory_space=pltpu.VMEM)
IN_HBM = pl.BlockSpec(memory_space=pltpu.HBM)


def in_hbm(array):
    return pltpu.with_memory_space_constraint(array, pltpu.HBM)


def kernel_call(kernel, out_shape, in_specs, out_specs, scratch, vmem_mib, flops, moved, alias=None):
    return pl.pallas_call(
        kernel,
        out_shape=out_shape,
        in_specs=in_specs,
        out_specs=out_specs,
        scratch_shapes=scratch,
        input_output_aliases=alias or {},
        compiler_params=pltpu.CompilerParams(vmem_limit_bytes=vmem_mib * MIB),
        cost_estimate=pl.CostEstimate(flops=flops, bytes_accessed=moved, transcendentals=0),
    )


def lanes_of(base, i):
    return pl.ds(pl.multiple_of(base + i * PAIR, PAIR), PAIR)


def two_blocks(first, second):
    top = jnp.concatenate([first, jnp.zeros(second.shape, second.dtype)], axis=1)
    bottom = jnp.concatenate([jnp.zeros(first.shape, first.dtype), second], axis=1)
    return jnp.concatenate([top, bottom], axis=0)


def score(a, b):
    return lax.dot_general(a, b, (((1,), (1,)), ((), ())), preferred_element_type=F32)


def tokens_dot(a, b):
    return lax.dot_general(a, b, (((0,), (0,)), ((), ())), preferred_element_type=F32)


AHEAD = 2


def half_cols(half):
    return pl.ds(pl.multiple_of(half * WIDTH, WIDTH), WIDTH)


def block_copies(k_hbm, v_hbm, k_buf, v_buf, sems, cols, n, slot, sem):
    rows = pl.ds(n * SPAN, SPAN)
    return (
        pltpu.make_async_copy(k_hbm.at[rows, cols], k_buf.at[slot], sems.at[0, sem]),
        pltpu.make_async_copy(v_hbm.at[rows, cols], v_buf.at[slot], sems.at[1, sem]),
    )


def add_state(n, count, k, v, o_ref, earlier_buf=None):
    for i in range(CHUNKS):
        pair = tokens_dot(k[:, i * PAIR : (i + 1) * PAIR], v[:, i * PAIR : (i + 1) * PAIR])
        for h in range(2):
            rows = slice(i * PAIR + h * DK, i * PAIR + (h + 1) * DK)
            state = pair[h * DK : (h + 1) * DK, h * DK : (h + 1) * DK]
            if n:
                state += o_ref[rows, :]
            o_ref[rows, :] = state
            if earlier_buf is not None and n < count - 1:
                earlier_buf[n, rows, :] = state.astype(BF16)


def states_of(blocks, copies, o_ref, earlier_hbm=None, earlier_buf=None, sems=None):
    count = len(blocks)
    outs = []
    for n, (k_buf, v_buf, slot) in enumerate(blocks):
        if n % 2 == 0:
            for copy in copies[n] + copies[n + 1]:
                copy.wait()
        add_state(n, count, k_buf[slot], v_buf[slot], o_ref, earlier_buf)
        if earlier_buf is not None and n < count - 1:
            outs.append(pltpu.make_async_copy(earlier_buf.at[n], earlier_hbm.at[n], sems.at[2, n]))
            outs[-1].start()
    for copy in outs:
        copy.wait()


def first_states_kernel(half_ref, k_hbm, v_hbm, o_ref, earlier_hbm, k_next, v_next, k_buf, v_buf, earlier_buf, sems):
    count = k_buf.shape[0]
    cols, next_cols = half_cols(half_ref[0]), half_cols(1 - half_ref[0])
    copies = [block_copies(k_hbm, v_hbm, k_buf, v_buf, sems, cols, n, n, n) for n in range(count)]
    ahead = [
        block_copies(k_hbm, v_hbm, k_next, v_next, sems, next_cols, n, n, count + n) for n in range(AHEAD)
    ]
    for pair in copies + ahead:
        for copy in pair:
            copy.start()
    states_of([(k_buf, v_buf, n) for n in range(count)], copies, o_ref, earlier_hbm, earlier_buf, sems)
    for pair in ahead:
        for copy in pair:
            copy.wait()


def second_states_kernel(half_ref, k_hbm, v_hbm, k_first, v_first, o_ref, k_buf, v_buf, sems):
    rest = k_buf.shape[0]
    cols = half_cols(half_ref[0])
    copies = [()] * AHEAD + [
        block_copies(k_hbm, v_hbm, k_buf, v_buf, sems, cols, AHEAD + n, n, n) for n in range(rest)
    ]
    for pair in copies:
        for copy in pair:
            copy.start()
    blocks = [(k_first, v_first, n) for n in range(AHEAD)] + [(k_buf, v_buf, n) for n in range(rest)]
    states_of(blocks, copies, o_ref)


def half_states(half, keys, values, ahead=None):
    tokens = keys.shape[0]
    count = tokens // SPAN
    first = ahead is None
    buf = pltpu.VMEM((count if first else count - AHEAD, SPAN, WIDTH), BF16)
    out_shape, out_specs = [jax.ShapeDtypeStruct((WIDTH, DK), F32)], [VMEM]
    scratch = [buf, buf, pltpu.SemaphoreType.DMA((3, count + AHEAD))]
    if first:
        out_shape += [pltpu.HBM((count - 1, WIDTH, DK), BF16)] + [pltpu.VMEM((AHEAD, SPAN, WIDTH), BF16)] * 2
        out_specs += [IN_HBM, VMEM, VMEM]
        scratch.insert(2, pltpu.VMEM((count - 1, WIDTH, DK), BF16))
    return kernel_call(
        first_states_kernel if first else second_states_kernel,
        out_shape,
        [SMEM, IN_HBM, IN_HBM] + [VMEM] * (0 if first else 2),
        out_specs,
        scratch,
        16,
        2 * tokens * HALF * DK * DK,
        4 * tokens * WIDTH,
    )(half, in_hbm(keys), in_hbm(values), *(ahead or ()))


def local_kernel(with_states, half_ref, q_hbm, k_hbm, v_hbm, *rest):
    if with_states:
        o_hbm, earlier_hbm, q_buf, k_buf, v_buf, o_buf, sems, sum_buf, earlier_buf = rest
    else:
        o_hbm, q_buf, k_buf, v_buf, o_buf, sems = rest
    base = half_ref[0] * WIDTH
    count = q_buf.shape[1] // SPAN
    rows = lax.broadcasted_iota(jnp.int32, (DK, PAIR), 0)
    cols = lax.broadcasted_iota(jnp.int32, (DK, PAIR), 1) % DK
    causal = rows >= cols

    def copies(i):
        lanes = lanes_of(base, i)
        return [
            pltpu.make_async_copy(hbm.at[:, lanes], buf.at[i], sems.at[j, i])
            for j, (hbm, buf) in enumerate(((q_hbm, q_buf), (k_hbm, k_buf), (v_hbm, v_buf)))
        ]

    def out_copies(i):
        lanes = lanes_of(0, i)
        outs = [pltpu.make_async_copy(o_buf.at[i], o_hbm.at[:, lanes], sems.at[3, i])]
        if with_states:
            outs.append(pltpu.make_async_copy(earlier_buf.at[i], earlier_hbm.at[:, lanes, :], sems.at[4, i]))
        return outs

    for i in range(CHUNKS):
        for copy in copies(i):
            copy.start()

    def chunk(i, carry):
        for copy in copies(i):
            copy.wait()

        def pairs_of(buf, n):
            rows = [buf[i, n * SPAN + j * DK : n * SPAN + (j + 1) * DK, :] for j in range(2)]
            return [two_blocks(r[:, :DK], r[:, DK:]) for r in rows]

        def scores_of(n):
            start = n * SPAN
            first_keys, second_keys = pairs_of(k_buf, n)
            top = score(q_buf[i, start : start + DK, :], first_keys)
            bottom = score(q_buf[i, start + DK : start + SPAN, :], first_keys)
            corner = score(q_buf[i, start + DK : start + SPAN, :], second_keys)
            return (
                jnp.where(causal, top, 0.0).astype(BF16),
                bottom.astype(BF16),
                jnp.where(causal, corner, 0.0).astype(BF16),
            )

        ready = scores_of(0)
        for n in range(count):
            top, bottom, corner = ready
            if n < count - 1:
                ready = scores_of(n + 1)
            first_values, second_values = pairs_of(v_buf, n)
            start = n * SPAN
            out_top = jnp.dot(top, first_values, preferred_element_type=F32)
            out_bottom = jnp.dot(bottom, first_values, preferred_element_type=F32)
            out_bottom += jnp.dot(corner, second_values, preferred_element_type=F32)
            o_buf[i, start : start + DK, :] = out_top.astype(BF16)
            o_buf[i, start + DK : start + SPAN, :] = out_bottom.astype(BF16)
            if with_states and n < count - 1:
                pair = tokens_dot(k_buf[i, start : start + SPAN, :], v_buf[i, start : start + SPAN, :])
                for h in range(2):
                    rows = slice(h * DK, (h + 1) * DK)
                    state = pair[rows, rows]
                    if n:
                        state += sum_buf[rows, :]
                    sum_buf[rows, :] = state
                    earlier_buf[i, n, rows, :] = state.astype(BF16)
        for copy in out_copies(i):
            copy.start()
        return carry

    lax.fori_loop(0, CHUNKS, chunk, 0)
    for i in range(CHUNKS):
        for copy in out_copies(i):
            copy.wait()


def local_part(half, queries, keys, values, with_states):
    tokens = queries.shape[0]
    earlier = tokens // SPAN - 1
    buf = pltpu.VMEM((CHUNKS, tokens, PAIR), BF16)
    out_shape, out_specs = [pltpu.HBM((tokens, WIDTH), BF16)], [IN_HBM]
    scratch = [buf, buf, buf, buf, pltpu.SemaphoreType.DMA((5, CHUNKS))]
    if with_states:
        out_shape.append(pltpu.HBM((earlier, WIDTH, DK), BF16))
        out_specs.append(IN_HBM)
        scratch += [pltpu.VMEM((PAIR, DK), F32), pltpu.VMEM((CHUNKS, earlier, PAIR, DK), BF16)]
    return kernel_call(
        functools.partial(local_kernel, with_states),
        out_shape,
        [SMEM, IN_HBM, IN_HBM, IN_HBM],
        out_specs,
        scratch,
        18,
        6 * tokens * WIDTH * SPAN,
        8 * tokens * WIDTH,
    )(half, in_hbm(queries), in_hbm(keys), in_hbm(values))


def scan_kernel(x_ref, o_ref):
    total = jnp.zeros(x_ref.shape[1:], F32)
    for j in range(x_ref.shape[0]):
        o_ref[j] = total
        total += x_ref[j]


def add_kernel(a_ref, b_ref, o_ref):
    o_ref[...] = a_ref[...] + b_ref[...]


def small_call(kernel, *args):
    shape, size = args[0].shape, args[0].size
    return kernel_call(kernel, pltpu.VMEM(shape, F32), [VMEM] * len(args), VMEM, [], 4, size, 12 * size)(*args)


def core_kernel(core_ref, chip_ref, mine_ref, theirs_ref, own_ref, partner_ref):
    first = chip_ref[...]

    @pl.when(core_ref[0] == 0)
    def _():
        own_ref[...] = first
        partner_ref[...] = first + mine_ref[...]

    @pl.when(core_ref[0] == 1)
    def _():
        own_ref[...] = first + theirs_ref[...]
        partner_ref[...] = first


def core_prefixes(core, before_chip, mine, theirs):
    size = before_chip.size
    return kernel_call(
        core_kernel,
        [jax.ShapeDtypeStruct(before_chip.shape, F32)] * 2,
        [SMEM, VMEM, VMEM, VMEM],
        [VMEM, VMEM],
        [],
        8,
        size,
        20 * size,
    )(core, before_chip, mine, theirs)


def output_kernel(half_ref, q_hbm, local_hbm, earlier_hbm, prefix_ref, gain_ref, *rest):
    o_hbm, q_buf, local_buf, earlier_buf, o_buf, sems = rest[-6:]
    base = half_ref[0] * WIDTH
    tokens = q_buf.shape[1]

    def copies(i):
        return (
            pltpu.make_async_copy(q_hbm.at[:, lanes_of(base, i)], q_buf.at[i], sems.at[0, i]),
            pltpu.make_async_copy(local_hbm.at[:, lanes_of(0, i)], local_buf.at[i], sems.at[1, i]),
            pltpu.make_async_copy(earlier_hbm.at[:, lanes_of(0, i), :], earlier_buf.at[i], sems.at[3, i]),
        )

    def out_copy(i):
        return pltpu.make_async_copy(o_buf.at[i], o_hbm.at[:, lanes_of(base, i)], sems.at[2, i])

    for i in range(CHUNKS):
        for copy in copies(i):
            copy.start()

    def chunk(i, carry):
        for copy in copies(i):
            copy.wait()
        prefix = prefix_ref[pl.ds(pl.multiple_of(i * PAIR, PAIR), PAIR), :]
        gain = gain_ref[:, lanes_of(base, i)] * DK**0.5
        spans = [slice(n * SPAN, (n + 1) * SPAN) for n in range(tokens // SPAN)]
        for n, span in enumerate(spans):
            carried = prefix + earlier_buf[i, n - 1].astype(F32) if n else prefix
            carried = carried.astype(BF16)
            carried = two_blocks(carried[:DK], carried[DK:])
            for part in (slice(span.start, span.start + DK), slice(span.start + DK, span.stop)):
                raw = local_buf[i, part, :] + jnp.dot(q_buf[i, part, :], carried, preferred_element_type=F32)
                for h in range(2):
                    lanes = slice(h * DK, (h + 1) * DK)
                    head = raw[:, lanes]
                    squares = jnp.sum(head * head, axis=-1, keepdims=True)
                    o_buf[i, part, lanes] = (head * lax.rsqrt(squares + DK * 1e-06) * gain[:, lanes]).astype(BF16)
        out_copy(i).start()
        return carry

    lax.fori_loop(0, CHUNKS, chunk, 0)
    for i in range(CHUNKS):
        out_copy(i).wait()


def half_output(half, queries, local, earlier, prefix, gain, partial):
    tokens, width = queries.shape
    in_specs = [SMEM, IN_HBM, IN_HBM, IN_HBM, VMEM, VMEM]
    args = [half, in_hbm(queries), in_hbm(local), in_hbm(earlier), prefix, gain]
    alias = {}
    if partial is not None:
        in_specs.append(IN_HBM)
        args.append(partial)
        alias = {6: 0}
    buf = pltpu.VMEM((CHUNKS, tokens, PAIR), BF16)
    return kernel_call(
        output_kernel,
        jax.ShapeDtypeStruct((tokens, width), BF16),
        in_specs,
        IN_HBM,
        [
            buf,
            buf,
            pltpu.VMEM((CHUNKS, earlier.shape[0], PAIR, DK), BF16),
            buf,
            pltpu.SemaphoreType.DMA((4, CHUNKS)),
        ],
        18,
        4 * tokens * WIDTH * DK,
        8 * tokens * WIDTH,
        alias,
    )(*args)


def shards(queries, keys, values, norm_gain):
    own = lax.axis_index("c").astype(jnp.int32).reshape(1)
    other = 1 - own
    chips = lax.axis_size("x") * lax.axis_size("y") * lax.axis_size("z")
    swap = functools.partial(lax.ppermute, axis_name="c", perm=[(0, 1), (1, 0)])
    others, earlier_other, *ahead = half_states(other, keys, values)
    theirs = swap(others)
    (mine,) = half_states(own, keys, values, ahead)
    chip = small_call(add_kernel, mine, theirs)
    pieces = lax.all_to_all(chip, CHIPS, 0, 0, tiled=True)
    (local_other,) = local_part(other, queries, keys, values, False)
    sums = small_call(scan_kernel, pieces.reshape(chips, -1, DK)).reshape(pieces.shape)
    before_chip = lax.all_to_all(sums, CHIPS, 0, 0, tiled=True)
    local_own, earlier_own = local_part(own, queries, keys, values, True)
    prefix_own, prefix_partner = core_prefixes(own, before_chip, mine, theirs)
    prefix_other = swap(prefix_partner)
    gain = norm_gain.reshape(1, -1)
    out = half_output(own, queries, local_own, earlier_own, prefix_own, gain, None)
    return half_output(other, queries, local_other, earlier_other, prefix_other, gain, out)


def solution(mesh):
    finer = Mesh(mesh.devices.reshape(4, 4, mesh.shape["inner"] // 2, 2), ALL)
    return jax.shard_map(
        shards, mesh=finer, in_specs=(P(ALL, None),) * 3 + (P(),), out_specs=P(ALL, None), check_vma=False
    )
```

time: 170 us -> 77.9 us (0.46)
  local copies, waits for them, and re-layouts: 50.5 us -> 0.01 us
  matrix products: 43.6 us -> 0 us
  Pallas kernels: 0 us -> 34.1 us
  waiting for transfers between devices: 18.7 us -> 0.01 us
  other arithmetic: 18.2 us -> 0 us
  blocking collectives: 22.2 us -> 38.9 us
  starting transfers between devices: 16.2 us -> 4.62 us
    dot_general x3 -> x0, matrix products: 43.6 us -> none  [the longest x1 19.4 us: shards(): jnp.einsum('nhcs,nshe->nche', scores, values_local, preferred_element_typ...]
    all_to_all x0 -> x2, blocking collectives: none -> 38.9 us  [the longest x1 23.2 us: shards(): pieces = lax.all_to_all(chip, CHIPS, 0, 0, tiled=True)]
    pallas_call x0 -> x9, Pallas kernels: none -> 34.1 us  [the longest x2 16.1 us: local_part(): kernel_call(functools.partial(local_kernel, with_states), out_shape, [SME...]
    unnamed x10 -> x2, local copies, waits for them, and re-layouts: 32.4 us -> 0.01 us
    all_gather x2 -> x0, blocking collectives: 22.2 us -> none  [carried_in(): pieces = lax.all_gather(subtotal, axis)]
    all_to_all x2 -> x0, waiting for transfers between devices: 18.7 us -> none  [the longest x1 15 us: shards(): lax.all_to_all(flat, 'inner', split_axis=1, concat_axis=0, tiled=True)]
    all_to_all x2 -> x0, starting transfers between devices: 16.2 us -> none  [the longest x1 9.38 us: shards(): lax.all_to_all(share_prefix, 'inner', split_axis=0, concat_axis=1, tiled=...]
    convert_element_type x1 -> x0, other arithmetic: 12 us -> none  [shards(): return normed.astype(jnp.bfloat16).reshape(tokens, H * DK)]
  transfers between devices with their start and end apart: 2 -> 2, of which waited for: 2 -> 0; matrix products, arithmetic and copies ran while one was open for 7% -> 0% of each run, Pallas kernels for 0% -> 31%
where the time goes in v2:
time: 77.9 us; the launch traced here: 77.7 us
  blocking collectives  38.9 us (50%)
  Pallas kernels  34.1 us (44%)
  starting transfers between devices  4.62 us (6%)
    all_to_all x1, blocking collectives, shards(): pieces = lax.all_to_all(chip, CHIPS, 0, 0, tiled=True)  23.2 us
    pallas_call x2, Pallas kernels, local_part(): kernel_call(functools.partial(local_kernel, with_states), out_shape, [SME...  16.1 us
    all_to_all x1, blocking collectives, shards(): before_chip = lax.all_to_all(sums, CHIPS, 0, 0, tiled=True)  15.7 us
    pallas_call x2, Pallas kernels, half_output(): kernel_call(output_kernel, jax.ShapeDtypeStruct((tokens, width), BF16), i...  10.7 us
    pallas_call x2, Pallas kernels, half_states(): kernel_call(first_states_kernel if first else second_states_kernel, out_s...  6.99 us
    ppermute x1, starting transfers between devices, shards(): prefix_other = swap(prefix_partner)  3.16 us
  transfers between devices with their start and end apart: 2, of which 0 were waited for; matrix products, arithmetic and copies ran while one was open for 0% of the time, Pallas kernels for 31%

profile of v2, /device:TPU:1, one launch (start us, length us, event | category | flops | bytes accessed | tf_op | source)
XLA Modules:
  0.0 77.7 jit_solution(2582887744597418138)
XLA Ops:
  0.0 4.0 %shard_map.47 = (f32[1024,128]{1,0:T(8,128)S(1)}, bf16[5,1024,128]{2,1,0:T(8,128)(2,1)}, bf16[2,256,1024]{2,1,0:T(8,128)(2,1)S(1)}, bf16[2,256,1024]{2,1,0:T(8,128)(2,1)S(1)}) custom-call(s32[1]{0:T(128)S(6)} %sub.3.half_ref, bf16[1536,2048]{1,0:T(8,128)(2,1)} %k_hbm.7, bf16[1536,2048]{1,0:T(8,128)(2,1)} %v_hbm.7), custom_call_target="tpu_custom_call" | custom-call | flops 402653184 | bytes 6291456 | tf_op jit(solution)/shard_map/pallas_call | solution.py:146
  4.1 1.5 %collective-permute-start = (f32[1024,128]{1,0:T(8,128)S(1)}, f32[1024,128]{1,0:T(8,128)S(1)}, u32[]{:S(2)}, u32[]{:S(2)}) collective-permute-start(f32[1024,128]{1,0:T(8,128)S(1)} %get-tuple-element.16), channel_id=1, source_target_pairs={{0,1},{1,0},{2,3},{3,2},{4,5},{5,4},{6,7},{7,6},{8,9},{9,8},{10,11... | collective-permute-start | bytes 1572872 | tf_op jit(solution)/shard_map/ppermute | solution.py:383
  5.5 2.9 %shard_map.48.a_ref.mine_ref = f32[1024,128]{1,0:T(8,128)S(1)} custom-call(s32[1]{0:T(128)} %bitcast.half_ref.core_ref, bf16[1536,2048]{1,0:T(8,128)(2,1)} %k_hbm.7, bf16[1536,2048]{1,0:T(8,128)(2,1)} %v_hbm.7, bf16[2,256,1024]{2,1,0:T(8,128)(2,1)S(1)} %get-tuple-element.14.k_first, bf16[2,256,1024]{2,1,0:T(8,128)(2,1)S(1)} %get-tuple-element.15.v_first), custom_call_target="tpu_custom_call" | custom-call | flops 402653184 | bytes 6291456 | tf_op jit(solution)/shard_map/pallas_call | solution.py:146
  8.5 0.0 collective-permute-done.b_ref.theirs_ref
  8.5 0.1 shard_map.49
  8.5 23.2 %all_to_all.17.x_ref = f32[64,16,128]{2,1,0:T(8,128)S(1)} all-to-all(f32[64,16,128]{2,1,0:T(8,128)S(1)} %bitcast.4), channel_id=1, replica_groups=mesh['x'=4,'y'=4,'z'=4,'c'=2] {'x','y','z'}, dimensions={0} | all-to-all | bytes 1048576 | tf_op jit(solution)/shard_map/all_to_all | solution.py:386
  31.8 0.1 shard_map.50
  31.8 15.7 %all_to_all.18 = f32[64,16,128]{2,1,0:T(8,128)S(1)} all-to-all(f32[64,16,128]{2,1,0:T(8,128)S(1)} %shard_map.50), channel_id=1, replica_groups=mesh['x'=4,'y'=4,'z'=4,'c'=2] {'x','y','z'}, dimensions={0} | all-to-all | bytes 1048576 | tf_op jit(solution)/shard_map/all_to_all | solution.py:389
  47.5 0.1 shard_map.51
  47.7 3.2 %collective-permute-start.1 = (f32[1024,128]{1,0:T(8,128)S(1)}, f32[1024,128]{1,0:T(8,128)S(1)}, u32[]{:S(2)}, u32[]{:S(2)}) collective-permute-start(f32[1024,128]{1,0:T(8,128)S(1)} %get-tuple-element.17), channel_id=1, source_target_pairs={{0,1},{1,0},{2,3},{3,2},{4,5},{5,4},{6,7},{7,6},{8,9},{9,8},{10,11... | collective-permute-start | bytes 1572872 | tf_op jit(solution)/shard_map/ppermute | solution.py:392
  50.8 7.8 %shard_map.46.local_hbm = bf16[1536,1024]{1,0:T(8,128)(2,1)} custom-call(s32[1]{0:T(128)S(6)} %sub.3.half_ref, bf16[1536,2048]{1,0:T(8,128)(2,1)} %q_hbm.7, bf16[1536,2048]{1,0:T(8,128)(2,1)} %k_hbm.7, bf16[1536,2048]{1,0:T(8,128)(2,1)} %v_hbm.7), custom_call_target="tpu_custom_call" | custom-call | flops 2415919104 | bytes 12582912 | tf_op jit(solution)/shard_map/pallas_call | solution.py:248
  58.6 0.0 copy-start
  58.6 8.3 %shard_map.52 = (bf16[1536,1024]{1,0:T(8,128)(2,1)}, bf16[5,1024,128]{2,1,0:T(8,128)(2,1)}) custom-call(s32[1]{0:T(128)} %bitcast.half_ref.core_ref, bf16[1536,2048]{1,0:T(8,128)(2,1)} %q_hbm.7, bf16[1536,2048]{1,0:T(8,128)(2,1)} %k_hbm.7, bf16[1536,2048]{1,0:T(8,128)(2,1)} %v_hbm.7), custom_call_target="tpu_custom_call" | custom-call | flops 2415919104 | bytes 12582912 | tf_op jit(solution)/shard_map/pallas_call | solution.py:248
  67.0 0.0 copy-done
  67.0 5.4 %shard_map.53.rest_0_ = bf16[1536,2048]{1,0:T(8,128)(2,1)} custom-call(s32[1]{0:T(128)} %bitcast.half_ref.core_ref, bf16[1536,2048]{1,0:T(8,128)(2,1)} %q_hbm.7, bf16[1536,1024]{1,0:T(8,128)(2,1)} %get-tuple-element.18.local_hbm, bf16[5,1024,128]{2,1,0:T(8,128)(2,1)} %get-tuple-element.19.earlier_hbm, f32[1024,128]{1,0:T(8,128)S(1)} %get-tuple-element.20.prefix_ref, ...), custom_call_target="tpu_custom_call" | custom-call | flops 805306368 | bytes 12582912 | tf_op jit(solution)/shard_map/pallas_call | solution.py:358
  72.3 0.0 collective-permute-done.1.prefix_ref
  72.4 5.4 %shard_map.54 = bf16[1536,2048]{1,0:T(8,128)(2,1)} custom-call(s32[1]{0:T(128)S(6)} %sub.3.half_ref, bf16[1536,2048]{1,0:T(8,128)(2,1)} %q_hbm.7, bf16[1536,1024]{1,0:T(8,128)(2,1)} %shard_map.46.local_hbm, bf16[5,1024,128]{2,1,0:T(8,128)(2,1)} %get-tuple-element.13.earlier_hbm, ...), custom_call_target="tpu_custom_call", output_to_operand_aliasing={{}: (6, {})} | custom-call | flops 805306368 | bytes 12582912 | tf_op jit(solution)/shard_map/pallas_call | solution.py:358
Async XLA Ops:
  4.1 4.4 %collective-permute-start = (f32[1024,128]{1,0:T(8,128)S(1)}, f32[1024,128]{1,0:T(8,128)S(1)}, u32[]{:S(2)}, u32[]{:S(2)}) collective-permute-start(f32[1024,128]{1,0:T(8,128)S(1)} %get-tuple-element.16), channel_id=1, source_target_pairs={{0,1},{1,0},{2,3},{3,2},{4,5},{5,4},{6,7},{7,6},{8,9},{9,8},{10,11... | collective-permute-start | bytes 1572872 | tf_op jit(solution)/shard_map/ppermute | solution.py:383
  47.7 24.7 %collective-permute-start.1 = (f32[1024,128]{1,0:T(8,128)S(1)}, f32[1024,128]{1,0:T(8,128)S(1)}, u32[]{:S(2)}, u32[]{:S(2)}) collective-permute-start(f32[1024,128]{1,0:T(8,128)S(1)} %get-tuple-element.17), channel_id=1, source_target_pairs={{0,1},{1,0},{2,3},{3,2},{4,5},{5,4},{6,7},{7,6},{8,9},{9,8},{10,11... | collective-permute-start | bytes 1572872 | tf_op jit(solution)/shard_map/ppermute | solution.py:392
  58.6 8.4 %copy-start = (f32[2048]{0:T(1024)S(1)}, f32[2048]{0:T(1024)}, u32[]{:S(2)}) copy-start(f32[2048]{0:T(1024)} %param.7) | copy-start | bytes 24580
